TPU v7x, 32 devices: a whole 2x2x4 slice. The times are simulated.
32 devices in a mesh: groups: 2 (over x), segment: 2 (over core), block: 8 (over z, y).
Axes of the slice: x: 2, y: 2, z: 4, core: 2. Of those that a mesh axis runs over, the one named last changes fastest.
Arguments:
- tokens: float32 [1024, 16384], P(('groups', 'segment'), 'block'), parts along dimension 0, may hold values from -32 to 32
- gains: float32 [2, 2, 16384], P('segment', None, 'block'), may hold values from 0.1 to 1.9
- right_factors: float32 [2, 2, 128, 128, 128], P('segment', None, 'block'), may hold values from -0.5 to 0.5
- left_factors: float32 [2, 2, 128, 128, 128], P('segment', None, 'block'), may hold values from -0.5 to 0.5
Outputs:
- output: float32 [1024, 16384], P(('groups', 'segment'), 'block'), parts along dimension 0
There are 2 independent parts, one for each index of `groups`. A program takes and returns all parts, laid end to end along the dimension named above; an argument that names none is the same for every part. Nothing has to cross between parts.
All inputs are finite; a program needn't handle non-finite values.
Results may differ from a plain program's by a relative error of at most 0.0003.
Values sent between devices are 32-bit elements; how exact they have to be, the bound alone decides.
A program may use at most 64 MiB of HBM per device.

v0:
```python
import jax
import jax.numpy as jnp
from jax import lax
from jax.sharding import PartitionSpec as P

D = 16384
epsilon = 1e-06
exact = lax.Precision.HIGH


def shifted(block, axis, distance):
    devices = range(lax.axis_size(axis))
    route = [((i - distance) % len(devices), i) for i in devices]
    return lax.ppermute(block, axis, route)


def apply_layer(current, gain_row, right_part, left_part):
    blocks_here = right_part.shape[0]
    block_size = right_part.shape[1]
    width_here, token_count = current.shape
    partial_squares = jnp.sum(current * current, axis=0)
    devices = lax.axis_size("block")
    copies = jnp.broadcast_to(partial_squares, (devices, token_count))
    sum_squares = lax.all_to_all(copies, "block", 0, 0, tiled=True).sum(axis=0)
    normed = current * lax.rsqrt(sum_squares / D + epsilon)[None, :] * gain_row[:, None]
    inner = jnp.einsum(
        "bit,bij->bjt",
        normed.reshape(blocks_here, block_size, token_count),
        right_part,
        precision=exact,
    )
    combined = jnp.einsum(
        "bjt,jbc->cjt",
        lax.all_to_all(inner, "block", split_axis=1, concat_axis=0, tiled=True),
        left_part,
        precision=exact,
    )
    mixed = lax.all_to_all(combined, "block", split_axis=0, concat_axis=1, tiled=True)
    return current + mixed.reshape(width_here, token_count) * jax.nn.silu(normed)


def body(tokens, gains, right_factors, left_factors):
    current = tokens.T
    rounds = right_factors.shape[1]
    segment_index = lax.axis_index("segment")
    own = (gains[0], right_factors[0], left_factors[0])
    other = [[shifted(part[r], "segment", 1) for part in own] for r in range(rounds)]
    for layer_index in range(2 * rounds):
        section, r = (layer_index % 2, layer_index // 2)
        chosen = [
            jnp.where(segment_index == section, mine[r], theirs)
            for mine, theirs in zip(own, other[r])
        ]
        current = apply_layer(current, *chosen)
    return current.T


def solution(mesh):
    placed = (
        P(("groups", "segment"), "block"),
        P("segment", None, "block"),
        P("segment", None, "block", None, None),
        P("segment", None, "block", None, None),
    )
    return jax.shard_map(
        body,
        mesh=mesh,
        in_specs=placed,
        out_specs=P(("groups", "segment"), "block"),
        check_vma=False,
    )
```

profile of v0, /device:TPU:0, one launch (start us, length us, event | category | flops | bytes accessed | tf_op | source)
XLA Modules:
  0.0 513.8 jit_solution(17633843209926145523)
XLA Ops:
  1.3 3.1 slice_bitcast_fusion
  7.3 7.3 %all-to-all-start = ((f32[8,1,256]{2,1,0:T(1,128)}), f32[8,1,256]{2,1,0:T(1,128)S(1)}, u32[]{:S(2)}, u32[]{:S(2)}) async-start(f32[8,1,256]{2,1,0:T(1,128)} %broadcast_in_dim.8), calls=%async_computation | async-start | bytes 16384 | tf_op jit(solution)/shard_map/all_to_all | solution.py:24
  14.6 6.5 %all-to-all-done = f32[8,1,256]{2,1,0:T(1,128)S(1)} async-done(((f32[8,1,256]{2,1,0:T(1,128)}), f32[8,1,256]{2,1,0:T(1,128)S(1)}, u32[]{:S(2)}, u32[]{:S(2)}) %all-to-all-start) | async-done | bytes 8224 | tf_op jit(solution)/shard_map/all_to_all | solution.py:24
  23.9 2.5 copy.120
  26.5 4.4 all-to-all-start.1
  30.8 3.1 slice_bitcast_fusion.1
  33.9 44.2 %all-to-all-done.1 = f32[16,128,256]{2,0,1:T(8,128)} async-done(((f32[16,128,256]{2,0,1:T(8,128)}), f32[16,128,256]{2,0,1:T(8,128)}, u32[]{:S(2)}, u32[]{:S(2)}) %all-to-all-start.1) | async-done | bytes 2097184 | tf_op jit(solution)/shard_map/all_to_all | solution.py:34
  82.8 53.1 %all_to_all.156 = f32[128,16,256]{2,1,0:T(8,128)S(1)} all-to-all(f32[128,16,256]{2,1,0:T(8,128)S(1)} %copy.123), channel_id=1, replica_groups=mesh['groups'=2,'segment'=2,'block'=8] {'block'}, dimensions={0} | all-to-all | bytes 4194304 | tf_op jit(solution)/shard_map/all_to_all | solution.py:38
  138.3 10.0 %all_to_all.157 = f32[8,1,256]{2,1,0:T(1,128)S(1)} all-to-all(f32[8,1,256]{2,1,0:T(1,128)S(1)} %broadcast_in_dim.9), channel_id=1, replica_groups=mesh['groups'=2,'segment'=2,'block'=8] {'block'}, dimensions={0} | all-to-all | bytes 16384 | tf_op jit(solution)/shard_map/all_to_all | solution.py:24
  153.0 49.9 %all_to_all.158 = f32[16,128,256]{2,0,1:T(8,128)S(1)} all-to-all(f32[16,128,256]{2,0,1:T(8,128)S(1)} %copy.127), channel_id=1, replica_groups=mesh['groups'=2,'segment'=2,'block'=8] {'block'}, dimensions={1} | all-to-all | bytes 4194304 | tf_op jit(solution)/shard_map/all_to_all | solution.py:34
  204.5 2.4 convolution_bitcast_fusion.2
  207.0 2.6 copy.130
  209.5 3.6 all-to-all-start.5
  213.7 46.0 %all-to-all-done.5 = f32[128,16,256]{2,1,0:T(8,128)S(1)} async-done(((f32[128,16,256]{2,1,0:T(8,128)}), f32[128,16,256]{2,1,0:T(8,128)S(1)}, u32[]{:S(2)}, u32[]{:S(2)}) %all-to-all-start.5) | async-done | bytes 2097184 | tf_op jit(solution)/shard_map/all_to_all | solution.py:38
  262.8 3.4 all-to-all-start.6
  266.2 6.5 %all-to-all-done.6 = f32[8,1,256]{2,1,0:T(1,128)S(1)} async-done(((f32[8,1,256]{2,1,0:T(1,128)}), f32[8,1,256]{2,1,0:T(1,128)S(1)}, u32[]{:S(2)}, u32[]{:S(2)}) %all-to-all-start.6) | async-done | bytes 8224 | tf_op jit(solution)/shard_map/all_to_all | solution.py:24
  275.6 2.5 copy.134
  278.1 4.4 all-to-all-start.7
  282.5 47.2 %all-to-all-done.7 = f32[16,128,256]{2,0,1:T(8,128)} async-done(((f32[16,128,256]{2,0,1:T(8,128)}), f32[16,128,256]{2,0,1:T(8,128)}, u32[]{:S(2)}, u32[]{:S(2)}) %all-to-all-start.7) | async-done | bytes 2097184 | tf_op jit(solution)/shard_map/all_to_all | solution.py:34
  334.4 53.1 %all_to_all.159 = f32[128,16,256]{2,1,0:T(8,128)S(1)} all-to-all(f32[128,16,256]{2,1,0:T(8,128)S(1)} %copy.137), channel_id=1, replica_groups=mesh['groups'=2,'segment'=2,'block'=8] {'block'}, dimensions={0} | all-to-all | bytes 4194304 | tf_op jit(solution)/shard_map/all_to_all | solution.py:38
  389.9 10.0 %all_to_all.160 = f32[8,1,256]{2,1,0:T(1,128)S(1)} all-to-all(f32[8,1,256]{2,1,0:T(1,128)S(1)} %broadcast_in_dim.11), channel_id=1, replica_groups=mesh['groups'=2,'segment'=2,'block'=8] {'block'}, dimensions={0} | all-to-all | bytes 16384 | tf_op jit(solution)/shard_map/all_to_all | solution.py:24
  404.7 49.9 %all_to_all.161 = f32[16,128,256]{2,0,1:T(8,128)S(1)} all-to-all(f32[16,128,256]{2,0,1:T(8,128)S(1)} %copy.141), channel_id=1, replica_groups=mesh['groups'=2,'segment'=2,'block'=8] {'block'}, dimensions={1} | all-to-all | bytes 4194304 | tf_op jit(solution)/shard_map/all_to_all | solution.py:34
  456.1 2.4 convolution_bitcast_fusion
  459.8 49.8 %all_to_all.162 = f32[128,16,256]{2,1,0:T(8,128)S(1)} all-to-all(f32[128,16,256]{2,1,0:T(8,128)S(1)} %copy.144), channel_id=1, replica_groups=mesh['groups'=2,'segment'=2,'block'=8] {'block'}, dimensions={0} | all-to-all | bytes 4194304 | tf_op jit(solution)/shard_map/all_to_all | solution.py:38
  (77 shorter events, 45.5 us)
Async XLA Ops:
  0.8 13.8 %collective-permute-start.2 = (f32[2048]{0:T(1024)S(1)}, f32[2048]{0:T(1024)S(1)}, u32[]{:S(2)}, u32[]{:S(2)}) collective-permute-start(f32[2048]{0:T(1024)S(1)} %bitcast.130), channel_id=1, source_target_pairs={{8,0},{0,8},{9,1},{1,9},{10,2},{2,10},{11,3},{3,11},{12,4},{4,12},... | collective-permute-start | bytes 24584 | tf_op jit(solution)/shard_map/ppermute | solution.py:14
  4.4 17.1 %collective-permute-start.1 = (f32[16,128,128]{2,1,0:T(8,128)}, f32[16,128,128]{2,1,0:T(8,128)S(1)}, u32[]{:S(2)}, u32[]{:S(2)}) collective-permute-start(f32[16,128,128]{2,1,0:T(8,128)} %get-tuple-element.14), channel_id=1, source_target_pairs={{8,0},{0,8},{9,1},{1,9},{10,2},{2,10},{11,3},{3,11},{12,4},{4,12},... | collective-permute-start | bytes 3145736 | tf_op jit(solution)/shard_map/ppermute | solution.py:14
  7.3 13.8 %all-to-all-start = ((f32[8,1,256]{2,1,0:T(1,128)}), f32[8,1,256]{2,1,0:T(1,128)S(1)}, u32[]{:S(2)}, u32[]{:S(2)}) async-start(f32[8,1,256]{2,1,0:T(1,128)} %broadcast_in_dim.8), calls=%async_computation | async-start | bytes 16384 | tf_op jit(solution)/shard_map/all_to_all | solution.py:24
  21.1 1.6 copy-start.1
  26.5 51.6 %all-to-all-start.1 = ((f32[16,128,256]{2,0,1:T(8,128)}), f32[16,128,256]{2,0,1:T(8,128)}, u32[]{:S(2)}, u32[]{:S(2)}) async-start(f32[16,128,256]{2,0,1:T(8,128)} %copy.120), calls=%async_computation.1 | async-start | bytes 4194304 | tf_op jit(solution)/shard_map/all_to_all | solution.py:34
  33.9 46.1 %collective-permute-start = (f32[16,128,128]{2,1,0:T(8,128)}, f32[16,128,128]{2,1,0:T(8,128)}, u32[]{:S(2)}, u32[]{:S(2)}) collective-permute-start(f32[16,128,128]{2,1,0:T(8,128)} %get-tuple-element.12), channel_id=1, source_target_pairs={{8,0},{0,8},{9,1},{1,9},{10,2},{2,10},{11,3},{3,11},{12,4},{4,12},... | collective-permute-start | bytes 3145736 | tf_op jit(solution)/shard_map/ppermute | solution.py:14
  78.1 2.2 copy-start.5
  148.4 2.2 copy-start.2
  202.9 1.6 copy-start.6
  209.5 50.2 %all-to-all-start.5 = ((f32[128,16,256]{2,1,0:T(8,128)}), f32[128,16,256]{2,1,0:T(8,128)S(1)}, u32[]{:S(2)}, u32[]{:S(2)}) async-start(f32[128,16,256]{2,1,0:T(8,128)} %copy.130), calls=%async_computation.5 | async-start | bytes 4194304 | tf_op jit(solution)/shard_map/all_to_all | solution.py:38
  213.1 53.1 %collective-permute-start.5 = (f32[2048]{0:T(1024)S(1)}, f32[2048]{0:T(1024)S(1)}, u32[]{:S(2)}, u32[]{:S(2)}) collective-permute-start(f32[2048]{0:T(1024)S(1)} %bitcast.128), channel_id=1, source_target_pairs={{8,0},{0,8},{9,1},{1,9},{10,2},{2,10},{11,3},{3,11},{12,4},{4,12},... | collective-permute-start | bytes 24584 | tf_op jit(solution)/shard_map/ppermute | solution.py:14
  213.2 59.9 %collective-permute-start.4 = (f32[16,128,128]{2,1,0:T(8,128)}, f32[16,128,128]{2,1,0:T(8,128)S(1)}, u32[]{:S(2)}, u32[]{:S(2)}) collective-permute-start(f32[16,128,128]{2,1,0:T(8,128)} %get-tuple-element.13), channel_id=1, source_target_pairs={{8,0},{0,8},{9,1},{1,9},{10,2},{2,10},{11,3},{3,11},{12,4},{4,12},... | collective-permute-start | bytes 3145736 | tf_op jit(solution)/shard_map/ppermute | solution.py:14
  259.7 1.6 copy-start
  262.8 9.9 %all-to-all-start.6 = ((f32[8,1,256]{2,1,0:T(1,128)}), f32[8,1,256]{2,1,0:T(1,128)S(1)}, u32[]{:S(2)}, u32[]{:S(2)}) async-start(f32[8,1,256]{2,1,0:T(1,128)} %broadcast_in_dim.10), calls=%async_computation.6 | async-start | bytes 16384 | tf_op jit(solution)/shard_map/all_to_all | solution.py:24
  272.8 1.6 copy-start.3
  278.1 51.6 %all-to-all-start.7 = ((f32[16,128,256]{2,0,1:T(8,128)}), f32[16,128,256]{2,0,1:T(8,128)}, u32[]{:S(2)}, u32[]{:S(2)}) async-start(f32[16,128,256]{2,0,1:T(8,128)} %copy.134), calls=%async_computation.7 | async-start | bytes 4194304 | tf_op jit(solution)/shard_map/all_to_all | solution.py:34
  282.5 49.2 %collective-permute-start.3 = (f32[16,128,128]{2,1,0:T(8,128)}, f32[16,128,128]{2,1,0:T(8,128)}, u32[]{:S(2)}, u32[]{:S(2)}) collective-permute-start(f32[16,128,128]{2,1,0:T(8,128)} %get-tuple-element.11), channel_id=1, source_target_pairs={{8,0},{0,8},{9,1},{1,9},{10,2},{2,10},{11,3},{3,11},{12,4},{4,12},... | collective-permute-start | bytes 3145736 | tf_op jit(solution)/shard_map/ppermute | solution.py:14
  329.7 2.2 copy-start.7
  400.0 2.2 copy-start.4
  454.6 1.6 copy-start.8
  509.6 1.6 copy-start.9
where the time goes:
time: 515 us; the launch traced here: 514 us
  blocking collectives  276 us (54%)
  waiting for transfers between devices  150 us (29%)
  local copies, waits for them, and re-layouts  39.6 us (8%)
  starting transfers between devices  24.2 us (5%)
  matrix products  12.1 us (2%)
  other arithmetic  11.3 us (2%)
    all_to_all x3, blocking collectives, apply_layer(): lax.all_to_all(combined, 'block', split_axis=0, concat_axis=1, tiled=True)  156 us
    all_to_all x2, blocking collectives, apply_layer(): lax.all_to_all(inner, 'block', split_axis=1, concat_axis=0, tiled=True)  99.8 us
    all_to_all x2, waiting for transfers between devices, apply_layer(): lax.all_to_all(inner, 'block', split_axis=1, concat_axis=0, tiled=True)  91.3 us
    all_to_all x1, waiting for transfers between devices, apply_layer(): lax.all_to_all(combined, 'block', split_axis=0, concat_axis=1, tiled=True)  46 us
    all_to_all x2, blocking collectives, apply_layer(): sum_squares = lax.all_to_all(copies, 'block', 0, 0, tiled=True).sum(axis=0)  20 us
    all_to_all x2, waiting for transfers between devices, apply_layer(): sum_squares = lax.all_to_all(copies, 'block', 0, 0, tiled=True).sum(axis=0)  13 us
    all_to_all x2, starting transfers between devices, apply_layer(): sum_squares = lax.all_to_all(copies, 'block', 0, 0, tiled=True).sum(axis=0)  10.7 us
    unnamed x21, local copies, waits for them, and re-layouts  10.7 us
  transfers between devices with their start and end apart: 11, of which 5 were waited for; matrix products, arithmetic and copies ran while one was open for 3% of the time, Pallas kernels for 0%

commit v1 on v0

--- a/solution.py
+++ b/solution.py
@@ -6,6 +6,17 @@
 D = 16384
 epsilon = 1e-06
 exact = lax.Precision.HIGH
+
+
+def split_up(array, dim, peers):
+    before, after = (array.shape[:dim], array.shape[dim + 1 :])
+    return jnp.moveaxis(array.reshape(*before, peers, -1, *after), dim, 0)
+
+
+def laid_out(tiles, dim):
+    tiles = jnp.moveaxis(tiles, 0, dim)
+    shape = tiles.shape
+    return tiles.reshape(*shape[:dim], shape[dim] * shape[dim + 1], *shape[dim + 2 :])
 
 
 def shifted(block, axis, distance):
@@ -35,7 +46,14 @@
         left_part,
         precision=exact,
     )
-    mixed = lax.all_to_all(combined, "block", split_axis=0, concat_axis=1, tiled=True)
+    size, here = (lax.axis_size("block"), lax.axis_index("block"))
+    blocks = split_up(combined, 0, size)
+    finished = [blocks[here]]
+    for step in range(1, size):
+        sent = blocks[here ^ step]
+        finished.append(lax.ppermute(sent, "block", [(i_2, i_2 ^ step) for i_2 in range(size)]))
+    blocks = jnp.stack(finished)[here ^ jnp.arange(size)]
+    mixed = laid_out(blocks, 1)
     return current + mixed.reshape(width_here, token_count) * jax.nn.silu(normed)
 
 

time: 515 us -> 531 us (1.031)
  blocking collectives: 276 us -> 134 us
  waiting for transfers between devices: 150 us -> 224 us
  starting transfers between devices: 24.2 us -> 68.5 us
  local copies, waits for them, and re-layouts: 39.6 us -> 77.1 us
    all_to_all x3 -> x0, blocking collectives: 156 us -> none  [apply_layer(): lax.all_to_all(combined, 'block', split_axis=0, concat_axis=1, tiled=True)]
    ppermute x0 -> x28, waiting for transfers between devices: none -> 120 us  [apply_layer(): lax.ppermute(sent, 'block', [(i_2, i_2 ^ step) for i_2 in range(size)])]
    all_to_all x1 -> x0, waiting for transfers between devices: 46 us -> none  [apply_layer(): lax.all_to_all(combined, 'block', split_axis=0, concat_axis=1, tiled=True)]
    ppermute x0 -> x28, starting transfers between devices: none -> 38.5 us  [apply_layer(): lax.ppermute(sent, 'block', [(i_2, i_2 ^ step) for i_2 in range(size)])]
    unnamed x21 -> x49, local copies, waits for them, and re-layouts: 10.7 us -> 31.5 us
    all_to_all x2, blocking collectives: 20 us -> 35.1 us  [apply_layer(): sum_squares = lax.all_to_all(copies, 'block', 0, 0, tiled=True).sum(axis=0)]
    gather x0 -> x4, local copies, waits for them, and re-layouts: none -> 11.8 us  [apply_layer(): blocks = jnp.stack(finished)[here ^ jnp.arange(size)]]
    all_to_all x2, starting transfers between devices: 10.7 us -> 19.8 us  [apply_layer(): sum_squares = lax.all_to_all(copies, 'block', 0, 0, tiled=True).sum(axis=0)]
  transfers between devices with their start and end apart: 11 -> 38, of which waited for: 5 -> 18; matrix products, arithmetic and copies ran while one was open for 3% -> 8% of each run, Pallas kernels for 0% -> 0%
where the time goes in v1:
time: 531 us; the launch traced here: 527 us
  waiting for transfers between devices  224 us (42%)
  blocking collectives  134 us (25%)
  local copies, waits for them, and re-layouts  77.1 us (15%)
  starting transfers between devices  68.5 us (13%)
  matrix products  12.1 us (2%)
  other arithmetic  11.3 us (2%)
    ppermute x28, waiting for transfers between devices, apply_layer(): lax.ppermute(sent, 'block', [(i_2, i_2 ^ step) for i_2 in range(size)])  120 us
    all_to_all x2, blocking collectives, apply_layer(): lax.all_to_all(inner, 'block', split_axis=1, concat_axis=0, tiled=True)  98.7 us
    all_to_all x2, waiting for transfers between devices, apply_layer(): lax.all_to_all(inner, 'block', split_axis=1, concat_axis=0, tiled=True)  91.1 us
    ppermute x28, starting transfers between devices, apply_layer(): lax.ppermute(sent, 'block', [(i_2, i_2 ^ step) for i_2 in range(size)])  38.5 us
    all_to_all x2, blocking collectives, apply_layer(): sum_squares = lax.all_to_all(copies, 'block', 0, 0, tiled=True).sum(axis=0)  35.1 us
    unnamed x49, local copies, waits for them, and re-layouts  31.5 us
    all_to_all x2, starting transfers between devices, apply_layer(): sum_squares = lax.all_to_all(copies, 'block', 0, 0, tiled=True).sum(axis=0)  19.8 us
    all_to_all x2, waiting for transfers between devices, apply_layer(): sum_squares = lax.all_to_all(copies, 'block', 0, 0, tiled=True).sum(axis=0)  13 us
  transfers between devices with their start and end apart: 38, of which 18 were waited for; matrix products, arithmetic and copies ran while one was open for 8% of the time, Pallas kernels for 0%

profile of v1, /device:TPU:0, one launch (start us, length us, event | category | flops | bytes accessed | tf_op | source)
XLA Modules:
  0.0 527.0 jit_solution(10918746640089043965)
XLA Ops:
  7.3 7.3 %all-to-all-start = ((f32[8,1,256]{2,1,0:T(1,128)}), f32[8,1,256]{2,1,0:T(1,128)S(1)}, u32[]{:S(2)}, u32[]{:S(2)}) async-start(f32[8,1,256]{2,1,0:T(1,128)} %broadcast_in_dim.8), calls=%async_computation | async-start | bytes 16384 | tf_op jit(solution)/shard_map/all_to_all | solution.py:35
  14.6 6.5 %all-to-all-done = f32[8,1,256]{2,1,0:T(1,128)S(1)} async-done(((f32[8,1,256]{2,1,0:T(1,128)}), f32[8,1,256]{2,1,0:T(1,128)S(1)}, u32[]{:S(2)}, u32[]{:S(2)}) %all-to-all-start) | async-done | bytes 8224 | tf_op jit(solution)/shard_map/all_to_all | solution.py:35
  26.5 4.4 all-to-all-start.1
  33.9 44.2 %all-to-all-done.1 = f32[16,128,256]{2,0,1:T(8,128)} async-done(((f32[16,128,256]{2,0,1:T(8,128)}), f32[16,128,256]{2,0,1:T(8,128)}, u32[]{:S(2)}, u32[]{:S(2)}) %all-to-all-start.1) | async-done | bytes 2097184 | tf_op jit(solution)/shard_map/all_to_all | solution.py:45
  87.3 3.8 collective-permute-start.7
  93.6 7.5 %collective-permute-done.4 = f32[16,16,256]{2,1,0:T(8,128)S(1)} collective-permute-done((f32[16,16,256]{2,1,0:T(8,128)S(1)}, f32[16,16,256]{2,1,0:T(8,128)S(1)}, u32[]{:S(2)}, u32[]{:S(2)}) %collective-permute-start.4) | collective-permute-done | bytes 262176 | tf_op jit(solution)/shard_map/ppermute | solution.py:54
  105.9 20.2 %collective-permute-done.7 = f32[16,16,256]{2,1,0:T(8,128)S(1)} collective-permute-done((f32[16,16,256]{2,1,0:T(8,128)S(1)}, f32[16,16,256]{2,1,0:T(8,128)S(1)}, u32[]{:S(2)}, u32[]{:S(2)}) %collective-permute-start.7) | collective-permute-done | bytes 262176 | tf_op jit(solution)/shard_map/ppermute | solution.py:54
  128.3 3.6 gather_fusion
  135.9 17.5 %all_to_all.96 = f32[8,1,256]{2,1,0:T(1,128)S(1)} all-to-all(f32[8,1,256]{2,1,0:T(1,128)S(1)} %broadcast_in_dim.9), channel_id=1, replica_groups=mesh['groups'=2,'segment'=2,'block'=8] {'block'}, dimensions={0} | all-to-all | bytes 16384 | tf_op jit(solution)/shard_map/all_to_all | solution.py:35
  158.1 49.3 %all_to_all.97 = f32[16,128,256]{2,0,1:T(8,128)S(1)} all-to-all(f32[16,128,256]{2,0,1:T(8,128)S(1)} %copy.214), channel_id=1, replica_groups=mesh['groups'=2,'segment'=2,'block'=8] {'block'}, dimensions={1} | all-to-all | bytes 4194304 | tf_op jit(solution)/shard_map/all_to_all | solution.py:45
  220.0 9.5 %collective-permute-done.11 = f32[16,16,256]{2,1,0:T(8,128)S(1)} collective-permute-done((f32[16,16,256]{2,1,0:T(8,128)S(1)}, f32[16,16,256]{2,1,0:T(8,128)S(1)}, u32[]{:S(2)}, u32[]{:S(2)}) %collective-permute-start.11) | collective-permute-done | bytes 262176 | tf_op jit(solution)/shard_map/ppermute | solution.py:54
  235.6 4.1 collective-permute-start.16
  240.4 16.2 %collective-permute-done.14 = f32[16,16,256]{2,1,0:T(8,128)S(1)} collective-permute-done((f32[16,16,256]{2,1,0:T(8,128)S(1)}, f32[16,16,256]{2,1,0:T(8,128)S(1)}, u32[]{:S(2)}, u32[]{:S(2)}) %collective-permute-start.14) | collective-permute-done | bytes 262176 | tf_op jit(solution)/shard_map/ppermute | solution.py:54
  264.1 12.6 %all-to-all-start.4 = ((f32[8,1,256]{2,1,0:T(1,128)}), f32[8,1,256]{2,1,0:T(1,128)S(1)}, u32[]{:S(2)}, u32[]{:S(2)}) async-start(f32[8,1,256]{2,1,0:T(1,128)} %broadcast_in_dim.10), calls=%async_computation.4 | async-start | bytes 16384 | tf_op jit(solution)/shard_map/all_to_all | solution.py:35
  276.7 6.5 %all-to-all-done.4 = f32[8,1,256]{2,1,0:T(1,128)S(1)} async-done(((f32[8,1,256]{2,1,0:T(1,128)}), f32[8,1,256]{2,1,0:T(1,128)S(1)}, u32[]{:S(2)}, u32[]{:S(2)}) %all-to-all-start.4) | async-done | bytes 8224 | tf_op jit(solution)/shard_map/all_to_all | solution.py:35
  288.6 4.6 all-to-all-start.5
  293.3 47.0 %all-to-all-done.5 = f32[16,128,256]{2,0,1:T(8,128)} async-done(((f32[16,128,256]{2,0,1:T(8,128)}), f32[16,128,256]{2,0,1:T(8,128)}, u32[]{:S(2)}, u32[]{:S(2)}) %all-to-all-start.5) | async-done | bytes 2097184 | tf_op jit(solution)/shard_map/all_to_all | solution.py:45
  355.7 7.5 %collective-permute-done.21 = f32[16,16,256]{2,1,0:T(8,128)S(1)} collective-permute-done((f32[16,16,256]{2,1,0:T(8,128)S(1)}, f32[16,16,256]{2,1,0:T(8,128)S(1)}, u32[]{:S(2)}, u32[]{:S(2)}) %collective-permute-start.21) | collective-permute-done | bytes 262176 | tf_op jit(solution)/shard_map/ppermute | solution.py:54
  368.2 20.1 %collective-permute-done.24 = f32[16,16,256]{2,1,0:T(8,128)S(1)} collective-permute-done((f32[16,16,256]{2,1,0:T(8,128)S(1)}, f32[16,16,256]{2,1,0:T(8,128)S(1)}, u32[]{:S(2)}, u32[]{:S(2)}) %collective-permute-start.24) | collective-permute-done | bytes 262176 | tf_op jit(solution)/shard_map/ppermute | solution.py:54
  398.0 17.6 %all_to_all.98 = f32[8,1,256]{2,1,0:T(1,128)S(1)} all-to-all(f32[8,1,256]{2,1,0:T(1,128)S(1)} %broadcast_in_dim.11), channel_id=1, replica_groups=mesh['groups'=2,'segment'=2,'block'=8] {'block'}, dimensions={0} | all-to-all | bytes 16384 | tf_op jit(solution)/shard_map/all_to_all | solution.py:35
  420.4 49.3 %all_to_all.99 = f32[16,128,256]{2,0,1:T(8,128)S(1)} all-to-all(f32[16,128,256]{2,0,1:T(8,128)S(1)} %copy.242), channel_id=1, replica_groups=mesh['groups'=2,'segment'=2,'block'=8] {'block'}, dimensions={1} | all-to-all | bytes 4194304 | tf_op jit(solution)/shard_map/all_to_all | solution.py:45
  485.7 5.5 %collective-permute-done.28 = f32[16,16,256]{2,1,0:T(8,128)S(1)} collective-permute-done((f32[16,16,256]{2,1,0:T(8,128)S(1)}, f32[16,16,256]{2,1,0:T(8,128)S(1)}, u32[]{:S(2)}, u32[]{:S(2)}) %collective-permute-start.28) | collective-permute-done | bytes 262176 | tf_op jit(solution)/shard_map/ppermute | solution.py:54
  494.7 17.1 %collective-permute-done.30 = f32[16,16,256]{2,1,0:T(8,128)S(1)} collective-permute-done((f32[16,16,256]{2,1,0:T(8,128)S(1)}, f32[16,16,256]{2,1,0:T(8,128)S(1)}, u32[]{:S(2)}, u32[]{:S(2)}) %collective-permute-start.30) | collective-permute-done | bytes 262176 | tf_op jit(solution)/shard_map/ppermute | solution.py:54
  512.5 5.9 %collective-permute-done.31 = f32[16,16,256]{2,1,0:T(8,128)S(1)} collective-permute-done((f32[16,16,256]{2,1,0:T(8,128)S(1)}, f32[16,16,256]{2,1,0:T(8,128)S(1)}, u32[]{:S(2)}, u32[]{:S(2)}) %collective-permute-start.31) | collective-permute-done | bytes 262176 | tf_op jit(solution)/shard_map/ppermute | solution.py:54
  (194 shorter events, 138.7 us)
Async XLA Ops:
  26.5 51.6 %all-to-all-start.1 = ((f32[16,128,256]{2,0,1:T(8,128)}), f32[16,128,256]{2,0,1:T(8,128)}, u32[]{:S(2)}, u32[]{:S(2)}) async-start(f32[16,128,256]{2,0,1:T(8,128)} %copy.200), calls=%async_computation.1 | async-start | bytes 4194304 | tf_op jit(solution)/shard_map/all_to_all | solution.py:45
  33.9 46.1 %collective-permute-start = (f32[16,128,128]{2,1,0:T(8,128)}, f32[16,128,128]{2,1,0:T(8,128)}, u32[]{:S(2)}, u32[]{:S(2)}) collective-permute-start(f32[16,128,128]{2,1,0:T(8,128)} %get-tuple-element.28), channel_id=1, source_target_pairs={{8,0},{0,8},{9,1},{1,9},{10,2},{2,10},{11,3},{3,11},{12,4},{4,12},... | collective-permute-start | bytes 3145736 | tf_op jit(solution)/shard_map/ppermute | solution.py:25
  84.7 19.8 %collective-permute-start.5 = (f32[16,16,256]{2,1,0:T(8,128)S(1)}, f32[16,16,256]{2,1,0:T(8,128)S(1)}, u32[]{:S(2)}, u32[]{:S(2)}) collective-permute-start(f32[16,16,256]{2,1,0:T(8,128)S(1)} %bitcast.285), channel_id=1, source_target_pairs={{0,3},{1,2},{2,1},{3,0},{4,7},{5,6},{6,5},{7,4},{8,11},{9,10},{10,... | collective-permute-start | bytes 786440 | tf_op jit(solution)/shard_map/ppermute | solution.py:54
  87.3 38.8 %collective-permute-start.7 = (f32[16,16,256]{2,1,0:T(8,128)S(1)}, f32[16,16,256]{2,1,0:T(8,128)S(1)}, u32[]{:S(2)}, u32[]{:S(2)}) collective-permute-start(f32[16,16,256]{2,1,0:T(8,128)S(1)} %bitcast.279), channel_id=1, source_target_pairs={{0,5},{1,4},{2,7},{3,6},{4,1},{5,0},{6,3},{7,2},{8,13},{9,12},{10,... | collective-permute-start | bytes 786440 | tf_op jit(solution)/shard_map/ppermute | solution.py:54
  91.4 35.5 %collective-permute-start.8 = (f32[16,16,256]{2,1,0:T(8,128)S(1)}, f32[16,16,256]{2,1,0:T(8,128)S(1)}, u32[]{:S(2)}, u32[]{:S(2)}) collective-permute-start(f32[16,16,256]{2,1,0:T(8,128)S(1)} %bitcast.276), channel_id=1, source_target_pairs={{0,6},{1,7},{2,4},{3,5},{4,2},{5,3},{6,0},{7,1},{8,14},{9,15},{10,... | collective-permute-start | bytes 786440 | tf_op jit(solution)/shard_map/ppermute | solution.py:54
  101.1 26.4 %collective-permute-start.9 = (f32[16,16,256]{2,1,0:T(8,128)S(1)}, f32[16,16,256]{2,1,0:T(8,128)S(1)}, u32[]{:S(2)}, u32[]{:S(2)}) collective-permute-start(f32[16,16,256]{2,1,0:T(8,128)S(1)} %bitcast.272), channel_id=1, source_target_pairs={{0,7},{1,6},{2,5},{3,4},{4,3},{5,2},{6,1},{7,0},{8,15},{9,14},{10,... | collective-permute-start | bytes 786440 | tf_op jit(solution)/shard_map/ppermute | solution.py:54
  213.4 63.3 %collective-permute-start.19 = (f32[2048]{0:T(1024)S(1)}, f32[2048]{0:T(1024)S(1)}, u32[]{:S(2)}, u32[]{:S(2)}) collective-permute-start(f32[2048]{0:T(1024)S(1)} %bitcast.298), channel_id=1, source_target_pairs={{8,0},{0,8},{9,1},{1,9},{10,2},{2,10},{11,3},{3,11},{12,4},{4,12},... | collective-permute-start | bytes 24584 | tf_op jit(solution)/shard_map/ppermute | solution.py:25
  213.4 70.2 %collective-permute-start.18 = (f32[16,128,128]{2,1,0:T(8,128)}, f32[16,128,128]{2,1,0:T(8,128)S(1)}, u32[]{:S(2)}, u32[]{:S(2)}) collective-permute-start(f32[16,128,128]{2,1,0:T(8,128)} %get-tuple-element.29), channel_id=1, source_target_pairs={{8,0},{0,8},{9,1},{1,9},{10,2},{2,10},{11,3},{3,11},{12,4},{4,12},... | collective-permute-start | bytes 3145736 | tf_op jit(solution)/shard_map/ppermute | solution.py:25
  215.2 18.4 %collective-permute-start.12 = (f32[16,16,256]{2,1,0:T(8,128)S(1)}, f32[16,16,256]{2,1,0:T(8,128)S(1)}, u32[]{:S(2)}, u32[]{:S(2)}) collective-permute-start(f32[16,16,256]{2,1,0:T(8,128)S(1)} %bitcast.294), channel_id=1, source_target_pairs={{0,3},{1,2},{2,1},{3,0},{4,7},{5,6},{6,5},{7,4},{8,11},{9,10},{10,... | collective-permute-start | bytes 786440 | tf_op jit(solution)/shard_map/ppermute | solution.py:54
  229.5 27.0 %collective-permute-start.14 = (f32[16,16,256]{2,1,0:T(8,128)S(1)}, f32[16,16,256]{2,1,0:T(8,128)S(1)}, u32[]{:S(2)}, u32[]{:S(2)}) collective-permute-start(f32[16,16,256]{2,1,0:T(8,128)S(1)} %bitcast.275), channel_id=1, source_target_pairs={{0,5},{1,4},{2,7},{3,6},{4,1},{5,0},{6,3},{7,2},{8,13},{9,12},{10,... | collective-permute-start | bytes 786440 | tf_op jit(solution)/shard_map/ppermute | solution.py:54
  233.6 23.7 %collective-permute-start.15 = (f32[16,16,256]{2,1,0:T(8,128)S(1)}, f32[16,16,256]{2,1,0:T(8,128)S(1)}, u32[]{:S(2)}, u32[]{:S(2)}) collective-permute-start(f32[16,16,256]{2,1,0:T(8,128)S(1)} %bitcast.271), channel_id=1, source_target_pairs={{0,6},{1,7},{2,4},{3,5},{4,2},{5,3},{6,0},{7,1},{8,14},{9,15},{10,... | collective-permute-start | bytes 786440 | tf_op jit(solution)/shard_map/ppermute | solution.py:54
  235.6 22.5 %collective-permute-start.16 = (f32[16,16,256]{2,1,0:T(8,128)S(1)}, f32[16,16,256]{2,1,0:T(8,128)S(1)}, u32[]{:S(2)}, u32[]{:S(2)}) collective-permute-start(f32[16,16,256]{2,1,0:T(8,128)S(1)} %bitcast.270), channel_id=1, source_target_pairs={{0,7},{1,6},{2,5},{3,4},{4,3},{5,2},{6,1},{7,0},{8,15},{9,14},{10,... | collective-permute-start | bytes 786440 | tf_op jit(solution)/shard_map/ppermute | solution.py:54
  264.1 19.1 %all-to-all-start.4 = ((f32[8,1,256]{2,1,0:T(1,128)}), f32[8,1,256]{2,1,0:T(1,128)S(1)}, u32[]{:S(2)}, u32[]{:S(2)}) async-start(f32[8,1,256]{2,1,0:T(1,128)} %broadcast_in_dim.10), calls=%async_computation.4 | async-start | bytes 16384 | tf_op jit(solution)/shard_map/all_to_all | solution.py:35
  288.6 51.6 %all-to-all-start.5 = ((f32[16,128,256]{2,0,1:T(8,128)}), f32[16,128,256]{2,0,1:T(8,128)}, u32[]{:S(2)}, u32[]{:S(2)}) async-start(f32[16,128,256]{2,0,1:T(8,128)} %copy.228), calls=%async_computation.5 | async-start | bytes 4194304 | tf_op jit(solution)/shard_map/all_to_all | solution.py:45
  293.2 49.0 %collective-permute-start.17 = (f32[16,128,128]{2,1,0:T(8,128)}, f32[16,128,128]{2,1,0:T(8,128)}, u32[]{:S(2)}, u32[]{:S(2)}) collective-permute-start(f32[16,128,128]{2,1,0:T(8,128)} %get-tuple-element.27), channel_id=1, source_target_pairs={{8,0},{0,8},{9,1},{1,9},{10,2},{2,10},{11,3},{3,11},{12,4},{4,12},... | collective-permute-start | bytes 3145736 | tf_op jit(solution)/shard_map/ppermute | solution.py:25
  346.8 19.9 %collective-permute-start.22 = (f32[16,16,256]{2,1,0:T(8,128)S(1)}, f32[16,16,256]{2,1,0:T(8,128)S(1)}, u32[]{:S(2)}, u32[]{:S(2)}) collective-permute-start(f32[16,16,256]{2,1,0:T(8,128)S(1)} %bitcast.286), channel_id=1, source_target_pairs={{0,3},{1,2},{2,1},{3,0},{4,7},{5,6},{6,5},{7,4},{8,11},{9,10},{10,... | collective-permute-start | bytes 786440 | tf_op jit(solution)/shard_map/ppermute | solution.py:54
  349.0 18.4 %collective-permute-start.23 = (f32[16,16,256]{2,1,0:T(8,128)S(1)}, f32[16,16,256]{2,1,0:T(8,128)S(1)}, u32[]{:S(2)}, u32[]{:S(2)}) collective-permute-start(f32[16,16,256]{2,1,0:T(8,128)S(1)} %bitcast.283), channel_id=1, source_target_pairs={{0,4},{1,5},{2,6},{3,7},{4,0},{5,1},{6,2},{7,3},{8,12},{9,13},{10,... | collective-permute-start | bytes 786440 | tf_op jit(solution)/shard_map/ppermute | solution.py:54
  349.6 38.7 %collective-permute-start.24 = (f32[16,16,256]{2,1,0:T(8,128)S(1)}, f32[16,16,256]{2,1,0:T(8,128)S(1)}, u32[]{:S(2)}, u32[]{:S(2)}) collective-permute-start(f32[16,16,256]{2,1,0:T(8,128)S(1)} %bitcast.280), channel_id=1, source_target_pairs={{0,5},{1,4},{2,7},{3,6},{4,1},{5,0},{6,3},{7,2},{8,13},{9,12},{10,... | collective-permute-start | bytes 786440 | tf_op jit(solution)/shard_map/ppermute | solution.py:54
  353.5 35.5 %collective-permute-start.25 = (f32[16,16,256]{2,1,0:T(8,128)S(1)}, f32[16,16,256]{2,1,0:T(8,128)S(1)}, u32[]{:S(2)}, u32[]{:S(2)}) collective-permute-start(f32[16,16,256]{2,1,0:T(8,128)S(1)} %bitcast.277), channel_id=1, source_target_pairs={{0,6},{1,7},{2,4},{3,5},{4,2},{5,3},{6,0},{7,1},{8,14},{9,15},{10,... | collective-permute-start | bytes 786440 | tf_op jit(solution)/shard_map/ppermute | solution.py:54
  363.3 26.4 %collective-permute-start.26 = (f32[16,16,256]{2,1,0:T(8,128)S(1)}, f32[16,16,256]{2,1,0:T(8,128)S(1)}, u32[]{:S(2)}, u32[]{:S(2)}) collective-permute-start(f32[16,16,256]{2,1,0:T(8,128)S(1)} %bitcast.273), channel_id=1, source_target_pairs={{0,7},{1,6},{2,5},{3,4},{4,3},{5,2},{6,1},{7,0},{8,15},{9,14},{10,... | collective-permute-start | bytes 786440 | tf_op jit(solution)/shard_map/ppermute | solution.py:54
  479.1 32.7 %collective-permute-start.30 = (f32[16,16,256]{2,1,0:T(8,128)S(1)}, f32[16,16,256]{2,1,0:T(8,128)S(1)}, u32[]{:S(2)}, u32[]{:S(2)}) collective-permute-start(f32[16,16,256]{2,1,0:T(8,128)S(1)} %bitcast.284), channel_id=1, source_target_pairs={{0,4},{1,5},{2,6},{3,7},{4,0},{5,1},{6,2},{7,3},{8,12},{9,13},{10,... | collective-permute-start | bytes 786440 | tf_op jit(solution)/shard_map/ppermute | solution.py:54
  480.4 38.0 %collective-permute-start.31 = (f32[16,16,256]{2,1,0:T(8,128)S(1)}, f32[16,16,256]{2,1,0:T(8,128)S(1)}, u32[]{:S(2)}, u32[]{:S(2)}) collective-permute-start(f32[16,16,256]{2,1,0:T(8,128)S(1)} %bitcast.281), channel_id=1, source_target_pairs={{0,5},{1,4},{2,7},{3,6},{4,1},{5,0},{6,3},{7,2},{8,13},{9,12},{10,... | collective-permute-start | bytes 786440 | tf_op jit(solution)/shard_map/ppermute | solution.py:54
  483.6 35.5 %collective-permute-start.32 = (f32[16,16,256]{2,1,0:T(8,128)S(1)}, f32[16,16,256]{2,1,0:T(8,128)S(1)}, u32[]{:S(2)}, u32[]{:S(2)}) collective-permute-start(f32[16,16,256]{2,1,0:T(8,128)S(1)} %bitcast.278), channel_id=1, source_target_pairs={{0,6},{1,7},{2,4},{3,5},{4,2},{5,3},{6,0},{7,1},{8,14},{9,15},{10,... | collective-permute-start | bytes 786440 | tf_op jit(solution)/shard_map/ppermute | solution.py:54
  491.3 28.5 %collective-permute-start.33 = (f32[16,16,256]{2,1,0:T(8,128)S(1)}, f32[16,16,256]{2,1,0:T(8,128)S(1)}, u32[]{:S(2)}, u32[]{:S(2)}) collective-permute-start(f32[16,16,256]{2,1,0:T(8,128)S(1)} %bitcast.274), channel_id=1, source_target_pairs={{0,7},{1,6},{2,5},{3,4},{4,3},{5,2},{6,1},{7,0},{8,15},{9,14},{10,... | collective-permute-start | bytes 786440 | tf_op jit(solution)/shard_map/ppermute | solution.py:54
  (24 other events, 216.5 us)
